TPU v7x, 32 devices: a whole 2x2x4 slice. The times are simulated.
32 devices in a mesh: outer: 8 (over z, x), inner: 4 (over y, core).
Axes of the slice: x: 2, y: 2, z: 4, core: 2. Of those that a mesh axis runs over, the one named last changes fastest.
Arguments:
- images: bfloat16 [32, 14, 14, 768], P(('outer', 'inner')), may hold values from -6 to 6
- cotangent: bfloat16 [32, 14, 14, 768], P(('outer', 'inner')), may hold values from -20 to 20
- conv_weight: float32 [7, 7, 768], replicated, may hold values from -0.875 to 0.875
- conv_bias: float32 [768], replicated, may hold values from -3 to 3
- norm_gain: float32 [768], replicated, may hold values from 0.1 to 1.9
- norm_bias: float32 [768], replicated, may hold values from -2 to 2
- expand_weight: bfloat16 [768, 3072], replicated, may hold values from -0.21875 to 0.21875
- expand_bias: float32 [3072], replicated, may hold values from -3 to 3
- reduce_weight: bfloat16 [3072, 768], replicated, may hold values from -0.109375 to 0.109375
- layer_scale: float32 [768], replicated, may hold values from 0.2 to 2
- right_first: float32 [3072, 32], replicated, may hold values from -5 to 5
- right_second: float32 [768, 32], replicated, may hold values from -5 to 5
Outputs:
- next_first: float32 [3072, 32], replicated
- next_second: float32 [768, 32], replicated
All inputs are finite; a program needn't handle non-finite values.
Results may differ from a plain program's by a relative error of at most 0.009.
Values may be sent and summed in bfloat16 or wider, within the bound.
No kernel may reach another device: no remote copies, remote signals or barrier semaphores. Data moves between devices by JAX's collectives and lax.ppermute only.
A program may use at most 64 MiB of HBM per device.

v0:
```python
import jax
import jax.numpy as jnp
from jax import lax
from jax.sharding import PartitionSpec as P


def depthwise(images, conv_weight, conv_bias):
    kernel = conv_weight.shape[0]
    margin = kernel // 2
    extent = images.shape[1]
    widened = jnp.pad(
        images.astype(jnp.float32), ((0, 0), (margin, margin), (margin, margin), (0, 0))
    )
    summed = jnp.zeros(images.shape, jnp.float32) + conv_bias
    for tap_row in range(kernel):
        for tap_col in range(kernel):
            summed = (
                summed
                + widened[:, tap_row : tap_row + extent, tap_col : tap_col + extent, :]
                * conv_weight[tap_row, tap_col]
            )
    return summed


def layer_norm(values, norm_gain, norm_bias):
    center = jnp.mean(values, axis=-1, keepdims=True)
    spread = jnp.mean((values - center) ** 2, axis=-1, keepdims=True)
    return ((values - center) * lax.rsqrt(spread + 1e-06) * norm_gain + norm_bias).astype(
        jnp.bfloat16
    )


def gelu_slope(hidden):
    return (
        0.5 * (1.0 + lax.erf(hidden * 0.7071067811865476))
        + hidden * jnp.exp(-0.5 * hidden * hidden) * 0.3989422804014327
    )


def project(rows_left, rows_right, right):
    thin = jnp.dot(
        rows_right, right.astype(jnp.bfloat16), preferred_element_type=jnp.float32
    ).astype(jnp.bfloat16)
    return lax.dot_general(
        rows_left, thin, (((0,), (0,)), ((), ())), preferred_element_type=jnp.float32
    )


def back_project(rows_left, rows_right, basis):
    rounded = basis.astype(jnp.bfloat16)
    thin = jnp.dot(rows_left, rounded, preferred_element_type=jnp.float32).astype(jnp.bfloat16)
    return lax.dot_general(
        rows_right, thin, (((0,), (0,)), ((), ())), preferred_element_type=jnp.float32
    )


def gram_of(partial_value):
    return lax.dot_general(
        partial_value, partial_value, (((0,), (0,)), ((), ())), precision=lax.Precision.HIGHEST
    )


def apply_factor(gram_matrix, partial_value):
    factor = jnp.linalg.cholesky(gram_matrix)
    return jax.scipy.linalg.solve_triangular(factor, partial_value.T, lower=True).T


def refine_layer(partial_value, rows_left, rows_right, scale):
    summed = lax.psum(partial_value, ("outer", "inner"))
    basis = apply_factor(gram_of(summed), summed)
    term = back_project(rows_left, rows_right, basis)
    return lax.psum(term, ("outer", "inner")) * scale


def shards(
    images,
    cotangent,
    conv_weight,
    conv_bias,
    norm_gain,
    norm_bias,
    expand_weight,
    expand_bias,
    reduce_weight,
    layer_scale,
    right_first,
    right_second,
):
    count = lax.axis_size("outer") * lax.axis_size("inner")
    scale = jnp.float32(1.0) / count
    width = images.shape[-1]
    conv_out = depthwise(images, conv_weight, conv_bias).reshape((-1, width))
    normed = layer_norm(conv_out, norm_gain, norm_bias)
    hidden = jnp.dot(normed, expand_weight, preferred_element_type=jnp.float32) + expand_bias
    activated = jax.nn.gelu(hidden, approximate=False).astype(jnp.bfloat16)
    out_grad = (cotangent.reshape((-1, width)).astype(jnp.float32) * layer_scale).astype(
        jnp.bfloat16
    )
    p_second = project(activated, out_grad, right_second)
    back = lax.dot_general(
        out_grad, reduce_weight, (((1,), (1,)), ((), ())), preferred_element_type=jnp.float32
    )
    hid_grad = (back * gelu_slope(hidden)).astype(jnp.bfloat16)
    p_first = project(normed, hid_grad, right_first)
    next_second = refine_layer(p_second, activated, out_grad, scale)
    next_first = refine_layer(p_first, normed, hid_grad, scale)
    return (next_first, next_second)


def solution(mesh):
    in_specs = (
        P(("outer", "inner"), None, None, None),
        P(("outer", "inner"), None, None, None),
        P(),
        P(),
        P(),
        P(),
        P(),
        P(),
        P(),
        P(),
        P(),
        P(),
    )
    out_specs = (P(), P())
    return jax.shard_map(shards, mesh=mesh, in_specs=in_specs, out_specs=out_specs, check_vma=False)
```

profile of v0, /device:TPU:0, one launch (start us, length us, event | category | flops | bytes accessed | tf_op | source)
XLA Modules:
  0.0 326.7 jit_solution(6438249491796293082)
XLA Ops:
  7.2 0.0 all-reduce.8.cloned.1.call-start
  7.2 1.1 slice_reduce_fusion.46
  8.3 1.4 slice_reduce_fusion.48
  9.7 0.0 copy-start.1
  9.7 1.4 slice_reduce_fusion.47
  11.1 1.0 convert_element_type.50
  12.1 0.0 copy-start.6
  12.1 0.0 copy-start.3
  12.1 0.0 copy-start.4
  12.1 0.0 copy-start.7
  12.2 6.3 %fusion.126 = (f32[14,14]{1,0:T(8,128)S(1)}, f32[1,14,14,768]{3,2,1,0:T(8,128)S(1)}) fusion(f32[768]{0:T(1024)S(1)} %get-tuple-element.50, f32[768]{0:T(1024)S(1)} %get-tuple-element.51, f32[768]{0:T(1024)S(1)} %get-tuple-element.4, f32[768]{0:T(1024)S(1)} %get-tuple-element.5, f32[768]{0:T(1024)S(1)} %get-tuple-element.6, f32[768]{0:T(1024)S(1)} %get-tuple-element.7, ...), kind=kLoop, calls=%fused_computation.256 | loop fusion | flops 14902076 | bytes 1358608 | tf_op jit(solution)/shard_map/reduce_sum | solution.py:26
  18.4 0.1 div.15
  18.5 0.2 multiply_reduce_fusion
  18.8 0.1 reshape.211
  18.8 0.0 copy-done.1
  18.9 0.1 reshape.212
  19.0 0.1 rsqrt.12
  19.0 0.0 copy-done.6
  19.0 0.0 copy-start.5
  19.1 0.0 slice-start
  19.1 0.0 copy-done.3
  19.1 0.0 copy-done.4
  19.1 0.0 copy-done.7
  19.1 0.0 slice-start.1
  19.2 8.0 %fusion.7 = (bf16[196,3072]{1,0:T(8,128)(2,1)S(1)}, f32[196,3072]{1,0:T(8,128)S(1)}) fusion(f32[3072]{0:T(1024)S(1)} %copy-done.7, bf16[768,3072]{1,0:T(8,128)(2,1)} %param.19, f32[196,768]{1,0:T(8,128)S(1)} %reshape.211, f32[768]{0:T(1024)S(1)} %copy-done.3, f32[768]{0:T(1024)S(1)} %copy-done.4, f32[196]{0:T(256)S(1)} %rsqrt.12, f32[196]{0:T(256)S(1)} %div.15), kind=kOutput, calls=%fused_computation.60 | convolution fusion | flops 965336064 | bytes 8953376 | tf_op jit(solution)/shard_map/dot_general | solution.py:94
  27.2 0.0 slice-done
  27.2 0.0 slice-done.1
  27.2 0.0 copy-start.2
  27.2 2.0 fusion
  29.2 0.0 copy-done.5
  29.2 2.4 fusion.15
  31.6 0.0 copy-done.2
  31.6 1.4 fusion.17
  33.1 0.0 all-reduce.8.cloned.1.call-update
  33.1 0.2 all-reduce.6.cloned.1.call-start
  33.3 130.9 %all-reduce.8.cloned.1.call-done = (f32[768,32]{0,1:T(8,128)}, f32[3072,32]{0,1:T(8,128)}) async-done(((f32[768,32]{0,1:T(8,128)}, f32[3072,32]{0,1:T(8,128)}), (f32[768,32]{0,1:T(8,128)}, f32[3072,32]{0,1:T(8,128)})) %all-reduce.8.cloned.1.call-update) | async-done | bytes 491536 | tf_op jit(solution)/shard_map/psum | solution.py:69
  164.2 0.0 copy-start
  164.2 1.3 fusion.128
  165.5 1.6 fusion.129
  167.0 0.1 copy.17
  167.1 2.9 cholesky.55
  170.1 0.6 compare_reduce_fusion
  170.7 0.7 fusion.121
  171.4 2.4 custom-call.11
  173.8 2.2 convolution_convert_fusion
  176.0 2.3 fusion.16
  178.3 0.1 copy.16
  178.4 2.9 cholesky.44
  181.3 0.6 compare_reduce_fusion.1
  182.0 0.7 fusion.120
  182.6 2.4 custom-call.10
  185.1 0.0 copy-done
  185.1 0.8 convolution_convert_fusion.1
  185.9 2.1 fusion.18
  188.0 0.0 all-reduce.6.cloned.1.call-update
  188.1 128.5 %all-reduce.6.cloned.1.call-done = (f32[3072,32]{0,1:T(8,128)}, f32[768,32]{0,1:T(8,128)}) async-done(((f32[3072,32]{0,1:T(8,128)}, f32[768,32]{0,1:T(8,128)}), (f32[3072,32]{0,1:T(8,128)}, f32[768,32]{0,1:T(8,128)})) %all-reduce.6.cloned.1.call-update) | async-done | bytes 491536 | tf_op jit(solution)/shard_map/psum | solution.py:72
  316.6 1.8 broadcast_multiply_fusion
  318.3 1.5 broadcast_multiply_fusion.1
  (8 shorter events, 0.1 us)
Async XLA Ops:
  7.2 157.0 %all-reduce.8.cloned.1.call-start = ((), (), s32[]{:S(2)}) async-start(), calls=%async_computation.1 | async-start | bytes 983040 | tf_op jit(solution)/shard_map/psum | solution.py:69
  9.7 9.2 %copy-start.1 = (bf16[1,14,14,768]{3,2,1,0:T(8,128)(2,1)S(1)}, bf16[1,14,14,768]{3,2,1,0:T(8,128)(2,1)}, u32[]{:S(2)}) copy-start(bf16[1,14,14,768]{3,2,1,0:T(8,128)(2,1)} %param.14) | copy-start | bytes 903172
  12.1 6.9 %copy-start.6 = (f32[768]{0:T(1024)S(1)}, f32[768]{0:T(1024)}, u32[]{:S(2)}) copy-start(f32[768]{0:T(1024)} %param.22) | copy-start | bytes 9220
  12.1 7.0 %copy-start.3 = (f32[768]{0:T(1024)S(1)}, f32[768]{0:T(1024)}, u32[]{:S(2)}) copy-start(f32[768]{0:T(1024)} %param.18) | copy-start | bytes 9220
  12.1 7.0 %copy-start.4 = (f32[768]{0:T(1024)S(1)}, f32[768]{0:T(1024)}, u32[]{:S(2)}) copy-start(f32[768]{0:T(1024)} %param.17) | copy-start | bytes 9220
  12.1 7.0 %copy-start.7 = (f32[3072]{0:T(1024)S(1)}, f32[3072]{0:T(1024)}, u32[]{:S(2)}) copy-start(f32[3072]{0:T(1024)} %param.20) | copy-start | bytes 36868
  19.0 10.2 %copy-start.5 = (f32[196]{0:T(256)}, f32[196]{0:T(256)S(1)}, u32[]{:S(2)}) copy-start(f32[196]{0:T(256)S(1)} %rsqrt.12) | copy-start | bytes 2356
  19.1 8.1 %slice-start = ((s8[4718592]{0:T(1024)(128)(4,1)}), s8[4194304]{0:T(1024)(128)(4,1)S(1)}, s32[]{:S(2)}) async-start(s8[4718592]{0:T(1024)(128)(4,1)} %bitcast.35), calls=%async_computation.2 | async-start | bytes 8388608
  19.1 8.1 %slice-start.1 = ((s8[4718592]{0:T(1024)(128)(4,1)}), s8[524288]{0:T(1024)(128)(4,1)S(1)}, s32[]{:S(2)}) async-start(s8[4718592]{0:T(1024)(128)(4,1)} %bitcast.35), calls=%async_computation.3 | async-start | bytes 1048576
  27.2 4.4 %copy-start.2 = (f32[768,32]{0,1:T(8,128)S(1)}, f32[768,32]{0,1:T(8,128)}, u32[]{:S(2)}) copy-start(f32[768,32]{0,1:T(8,128)} %param.24) | copy-start | bytes 294916
  33.1 283.5 %all-reduce.6.cloned.1.call-start = ((), (), s32[]{:S(2)}) async-start(), calls=%async_computation | async-start | bytes 983040 | tf_op jit(solution)/shard_map/psum | solution.py:72
  164.2 20.9 %copy-start = (f32[768,32]{0,1:T(8,128)S(1)}, f32[768,32]{0,1:T(8,128)}, u32[]{:S(2)}) copy-start(f32[768,32]{0,1:T(8,128)} %get-tuple-element.54) | copy-start | bytes 294916
Sparse Core Ops, SparseCore 0:
  33.2 130.9 all-reduce.7
  188.2 128.3 all-reduce.5
where the time goes:
time: 327 us
  waiting for transfers between devices  259 us (79%)
  other arithmetic  24.2 us (7%)
  matrix products  24.1 us (7%)
  between operations  14.3 us (4%)
  local copies, waits for them, and re-layouts  4.39 us (1%)
    psum x1, waiting for transfers between devices, refine_layer(): summed = lax.psum(partial_value, ('outer', 'inner'))  131 us
    psum x1, waiting for transfers between devices, refine_layer(): return lax.psum(term, ('outer', 'inner')) * scale  129 us
    dot_general x1, matrix products, shards(): jnp.dot(normed, expand_weight, preferred_element_type=jnp.float32)  8.02 us
    another operation x6, other arithmetic, apply_factor(): factor = jnp.linalg.cholesky(gram_matrix)  7.19 us
  transfers between devices with their start and end apart: 2, of which 2 were waited for; matrix products, arithmetic and copies ran while one was open for 0% of the time, Pallas kernels for 0%

commit v1 on v0

--- a/solution.py
+++ b/solution.py
@@ -2,6 +2,12 @@
 import jax.numpy as jnp
 from jax import lax
 from jax.sharding import PartitionSpec as P
+from jax.lax import psum
+
+
+def define_the_clusters(frame_in):
+    arr_now = psum(psum(frame_in, axis_name="inner"), axis_name="outer")
+    return arr_now
 
 
 def depthwise(images, conv_weight, conv_bias):
@@ -69,7 +75,7 @@
     summed = lax.psum(partial_value, ("outer", "inner"))
     basis = apply_factor(gram_of(summed), summed)
     term = back_project(rows_left, rows_right, basis)
-    return lax.psum(term, ("outer", "inner")) * scale
+    return define_the_clusters(term) * scale
 
 
 def shards(

time: 327 us -> 308 us (0.942)
  waiting for transfers between devices: 259 us -> 241 us
    psum x1 -> x2, waiting for transfers between devices: 129 us -> 110 us  [define_the_clusters(): arr_now = psum(psum(frame_in, axis_name='inner'), axis_name='outer')]
  transfers between devices with their start and end apart: 2 -> 3, of which waited for: 2 -> 3; matrix products, arithmetic and copies ran while one was open for 0% -> 0% of each run, Pallas kernels for 0% -> 0%
where the time goes in v1:
time: 308 us
  waiting for transfers between devices  241 us (78%)
  other arithmetic  24.2 us (8%)
  matrix products  24.1 us (8%)
  between operations  14 us (5%)
  local copies, waits for them, and re-layouts  4.39 us (1%)
    psum x1, waiting for transfers between devices, refine_layer(): summed = lax.psum(partial_value, ('outer', 'inner'))  131 us
    psum x2, waiting for transfers between devices, define_the_clusters(): arr_now = psum(psum(frame_in, axis_name='inner'), axis_name='outer')  110 us
    dot_general x1, matrix products, shards(): jnp.dot(normed, expand_weight, preferred_element_type=jnp.float32)  8.02 us
    another operation x6, other arithmetic, apply_factor(): factor = jnp.linalg.cholesky(gram_matrix)  7.19 us
    reduce_sum x1, other arithmetic, layer_norm(): center = jnp.mean(values, axis=-1, keepdims=True)  6.22 us
    another operation x4, other arithmetic, apply_factor(): jax.scipy.linalg.solve_triangular(factor, partial_value.T, lower=True)  6.17 us
  transfers between devices with their start and end apart: 3, of which 3 were waited for; matrix products, arithmetic and copies ran while one was open for 0% of the time, Pallas kernels for 0%

profile of v1, /device:TPU:0, one launch (start us, length us, event | category | flops | bytes accessed | tf_op | source)
XLA Modules:
  0.0 307.8 jit_solution(3893757241460512935)
XLA Ops:
  7.2 0.0 all-reduce.8.cloned.1.call-start
  7.2 1.1 slice_reduce_fusion.46
  8.3 1.4 slice_reduce_fusion.48
  9.7 0.0 copy-start.1
  9.7 1.4 slice_reduce_fusion.47
  11.1 1.0 convert_element_type.50
  12.1 0.0 copy-start.6
  12.1 0.0 copy-start.3
  12.1 0.0 copy-start.4
  12.1 0.0 copy-start.7
  12.2 6.2 %fusion.126 = (f32[14,14]{1,0:T(8,128)S(1)}, f32[1,14,14,768]{3,2,1,0:T(8,128)S(1)}) fusion(f32[768]{0:T(1024)S(1)} %get-tuple-element.50, f32[768]{0:T(1024)S(1)} %get-tuple-element.51, f32[768]{0:T(1024)S(1)} %get-tuple-element.4, f32[768]{0:T(1024)S(1)} %get-tuple-element.5, f32[768]{0:T(1024)S(1)} %get-tuple-element.6, f32[768]{0:T(1024)S(1)} %get-tuple-element.7, ...), kind=kLoop, calls=%fused_computation.256 | loop fusion | flops 14902076 | bytes 1358608 | tf_op jit(solution)/shard_map/reduce_sum | solution.py:32
  18.4 0.1 div.15
  18.5 0.2 multiply_reduce_fusion
  18.7 0.1 reshape.211
  18.8 0.0 copy-done.1
  18.8 0.1 reshape.212
  18.9 0.1 rsqrt.12
  19.0 0.0 copy-done.6
  19.0 0.0 copy-start.5
  19.0 0.0 slice-start
  19.1 0.0 copy-done.3
  19.1 0.0 copy-done.4
  19.1 0.0 copy-done.7
  19.1 0.0 slice-start.1
  19.1 8.0 %fusion.7 = (bf16[196,3072]{1,0:T(8,128)(2,1)S(1)}, f32[196,3072]{1,0:T(8,128)S(1)}) fusion(f32[3072]{0:T(1024)S(1)} %copy-done.7, bf16[768,3072]{1,0:T(8,128)(2,1)} %param.19, f32[196,768]{1,0:T(8,128)S(1)} %reshape.211, f32[768]{0:T(1024)S(1)} %copy-done.3, f32[768]{0:T(1024)S(1)} %copy-done.4, f32[196]{0:T(256)S(1)} %rsqrt.12, f32[196]{0:T(256)S(1)} %div.15), kind=kOutput, calls=%fused_computation.60 | convolution fusion | flops 965336064 | bytes 8953376 | tf_op jit(solution)/shard_map/dot_general | solution.py:100
  27.2 0.0 slice-done
  27.2 0.0 slice-done.1
  27.2 0.0 copy-start.2
  27.2 2.0 fusion
  29.2 0.0 copy-done.5
  29.2 2.4 fusion.15
  31.6 0.0 copy-done.2
  31.6 1.4 fusion.17
  33.0 0.0 all-reduce.8.cloned.1.call-update
  33.1 0.0 all-reduce.12.cloned.1.call-start
  33.1 131.1 %all-reduce.8.cloned.1.call-done = (f32[768,32]{0,1:T(8,128)}, f32[3072,32]{0,1:T(8,128)}) async-done(((f32[768,32]{0,1:T(8,128)}, f32[3072,32]{0,1:T(8,128)}), (f32[768,32]{0,1:T(8,128)}, f32[3072,32]{0,1:T(8,128)})) %all-reduce.8.cloned.1.call-update) | async-done | bytes 491536 | tf_op jit(solution)/shard_map/psum | solution.py:75
  164.3 0.0 copy-start
  164.3 1.3 fusion.128
  165.5 1.6 fusion.129
  167.1 0.1 copy.17
  167.2 2.9 cholesky.55
  170.1 0.6 compare_reduce_fusion
  170.8 0.7 fusion.121
  171.4 2.4 custom-call.11
  173.9 2.2 convolution_convert_fusion
  176.1 2.3 fusion.16
  178.4 0.1 copy.16
  178.4 2.9 cholesky.44
  181.4 0.6 compare_reduce_fusion.1
  182.0 0.7 fusion.120
  182.7 2.4 custom-call.10
  185.1 0.0 copy-done
  185.1 0.8 convolution_convert_fusion.1
  186.0 2.1 fusion.18
  188.1 0.0 all-reduce.12.cloned.1.call-update
  188.1 0.0 all-reduce.10.cloned.1.call-start
  188.2 33.7 %all-reduce.12.cloned.1.call-done = (f32[3072,32]{0,1:T(8,128)}, f32[768,32]{0,1:T(8,128)}) async-done(((f32[3072,32]{0,1:T(8,128)}, f32[768,32]{0,1:T(8,128)}), (f32[3072,32]{0,1:T(8,128)}, f32[768,32]{0,1:T(8,128)})) %all-reduce.12.cloned.1.call-update) | async-done | bytes 491536 | tf_op jit(solution)/shard_map/psum | solution.py:9
  221.9 0.0 all-reduce.10.cloned.1.call-update
  221.9 76.1 %all-reduce.10.cloned.1.call-done = (f32[3072,32]{0,1:T(8,128)}, f32[768,32]{0,1:T(8,128)}) async-done(((f32[3072,32]{0,1:T(8,128)}, f32[768,32]{0,1:T(8,128)}), (f32[3072,32]{0,1:T(8,128)}, f32[768,32]{0,1:T(8,128)})) %all-reduce.10.cloned.1.call-update) | async-done | bytes 491536 | tf_op jit(solution)/shard_map/psum | solution.py:9
  298.0 1.8 broadcast_multiply_fusion
  299.8 1.5 broadcast_multiply_fusion.1
  (8 shorter events, 0.1 us)
Async XLA Ops:
  7.2 157.1 %all-reduce.8.cloned.1.call-start = ((), (), s32[]{:S(2)}) async-start(), calls=%async_computation | async-start | bytes 983040 | tf_op jit(solution)/shard_map/psum | solution.py:75
  9.7 9.1 %copy-start.1 = (bf16[1,14,14,768]{3,2,1,0:T(8,128)(2,1)S(1)}, bf16[1,14,14,768]{3,2,1,0:T(8,128)(2,1)}, u32[]{:S(2)}) copy-start(bf16[1,14,14,768]{3,2,1,0:T(8,128)(2,1)} %param.14) | copy-start | bytes 903172
  12.1 6.9 %copy-start.6 = (f32[768]{0:T(1024)S(1)}, f32[768]{0:T(1024)}, u32[]{:S(2)}) copy-start(f32[768]{0:T(1024)} %param.22) | copy-start | bytes 9220
  12.1 7.0 %copy-start.3 = (f32[768]{0:T(1024)S(1)}, f32[768]{0:T(1024)}, u32[]{:S(2)}) copy-start(f32[768]{0:T(1024)} %param.18) | copy-start | bytes 9220
  12.1 7.0 %copy-start.4 = (f32[768]{0:T(1024)S(1)}, f32[768]{0:T(1024)}, u32[]{:S(2)}) copy-start(f32[768]{0:T(1024)} %param.17) | copy-start | bytes 9220
  12.1 7.0 %copy-start.7 = (f32[3072]{0:T(1024)S(1)}, f32[3072]{0:T(1024)}, u32[]{:S(2)}) copy-start(f32[3072]{0:T(1024)} %param.20) | copy-start | bytes 36868
  19.0 10.2 %copy-start.5 = (f32[196]{0:T(256)}, f32[196]{0:T(256)S(1)}, u32[]{:S(2)}) copy-start(f32[196]{0:T(256)S(1)} %rsqrt.12) | copy-start | bytes 2356
  19.0 8.1 %slice-start = ((s8[4718592]{0:T(1024)(128)(4,1)}), s8[4194304]{0:T(1024)(128)(4,1)S(1)}, s32[]{:S(2)}) async-start(s8[4718592]{0:T(1024)(128)(4,1)} %bitcast.35), calls=%async_computation.3 | async-start | bytes 8388608
  19.1 8.1 %slice-start.1 = ((s8[4718592]{0:T(1024)(128)(4,1)}), s8[524288]{0:T(1024)(128)(4,1)S(1)}, s32[]{:S(2)}) async-start(s8[4718592]{0:T(1024)(128)(4,1)} %bitcast.35), calls=%async_computation.4 | async-start | bytes 1048576
  27.2 4.4 %copy-start.2 = (f32[768,32]{0,1:T(8,128)S(1)}, f32[768,32]{0,1:T(8,128)}, u32[]{:S(2)}) copy-start(f32[768,32]{0,1:T(8,128)} %param.24) | copy-start | bytes 294916
  33.1 188.8 %all-reduce.12.cloned.1.call-start = ((), (), s32[]{:S(2)}) async-start(), calls=%async_computation.2 | async-start | bytes 983040 | tf_op jit(solution)/shard_map/psum | solution.py:9
  164.3 20.9 %copy-start = (f32[768,32]{0,1:T(8,128)S(1)}, f32[768,32]{0,1:T(8,128)}, u32[]{:S(2)}) copy-start(f32[768,32]{0,1:T(8,128)} %get-tuple-element.52) | copy-start | bytes 294916
  188.1 109.9 %all-reduce.10.cloned.1.call-start = ((), (), s32[]{:S(2)}) async-start(), calls=%async_computation.1 | async-start | bytes 983040 | tf_op jit(solution)/shard_map/psum | solution.py:9
Sparse Core Ops, SparseCore 0:
  33.2 131.0 all-reduce.7
  188.2 33.5 all-reduce.11
  225.3 72.6 all-reduce.9
